TPU v7x, 256 devices: a whole 4x4x8 slice. The times are simulated.
256 devices in a mesh: dom: 32 (over x, z), grp: 8 (over y, core).
Axes of the slice: x: 4, y: 4, z: 8, core: 2. Of those that a mesh axis runs over, the one named last changes fastest.
Arguments:
- node_feats: bfloat16 [65536, 1024], P(('dom', 'grp')), may hold values from -6 to 6
- weight: bfloat16 [1024, 512], replicated, may hold values from -0.1875 to 0.1875
- bias: float32 [512], replicated, may hold values from -4 to 4
- cotangent: bfloat16 [65536, 512], P(('dom', 'grp')), may hold values from -6 to 6
- tile_bank: bfloat16 [16, 128, 128], replicated, may hold values from -0.125 to 0.125
- local_cols: int32 [32, 16, 16], P('dom'), may hold values from 0 to 15
- local_banks: int32 [32, 16, 16], P('dom'), may hold values from 0 to 15
- published: int32 [32, 4], P('dom'), may hold values from 0 to 15, as said below
- send_table: int32 [32, 32, 2], replicated, may hold values from -1 to 3, as said below
- halo_rows: int32 [32, 32, 2], P('dom'), may hold values from 0 to 15
- halo_banks: int32 [32, 32, 2], P('dom'), may hold values from 0 to 15
Outputs:
- activations: bfloat16 [65536, 512], P(('dom', 'grp'))
- grad_nodes: bfloat16 [65536, 1024], P(('dom', 'grp'))
- grad_weight: float32 [1024, 512], replicated
- grad_bias: float32 [512], replicated
Inputs may be any that keep to these rules, and one draw needn't show every extreme that they name: `published`: the 4 entries of a partition are distinct block numbers of that partition; 0 and 15 each appear in some partition's list. `send_table`: entry s of the pair (src, p) is -1 or an index into the offered list of src; the live entries of a pair come first and are distinct; a pair (p, p) has none; some pair has all 2 entries live.
All inputs are finite; a program needn't handle non-finite values.
Results may differ from a plain program's by a relative error of at most 0.019.
The roundings to bfloat16 on the way count: a program that leaves them out, or rounds other values in their place, can miss the bound.
Values may be sent and summed in bfloat16 or wider, within the bound.
A program may use at most 64 MiB of HBM per device.

v0:
```python
import jax
import jax.numpy as jnp
from jax import lax
from jax.sharding import PartitionSpec as P


def per_device(
    node_feats,
    weight,
    bias,
    cotangent,
    tile_bank,
    local_cols,
    local_banks,
    published,
    send_table,
    halo_rows,
    halo_banks,
):
    domains = lax.axis_size("dom")
    groups = lax.axis_size("grp")
    domain_index = lax.axis_index("dom")
    rows_here = node_feats.shape[0]
    tile_size = tile_bank.shape[1]
    slot_count = send_table.shape[2]
    pub_count = published.shape[1]
    tiles_row = local_cols.shape[2]
    features = lax.all_to_all(node_feats, "grp", split_axis=1, concat_axis=0, tiled=True)
    part_rows, narrow = features.shape
    blocks = part_rows // tile_size
    feat_blocks = features.reshape(blocks, tile_size, narrow)
    cols_here = local_cols[0]
    banks_here = local_banks[0]
    own_pub = published[0]
    incoming = lax.dynamic_index_in_dim(send_table, domain_index, 1, keepdims=False)
    live_in = (incoming >= 0).astype(jnp.float32)[:, :, None, None]
    rows_in = halo_rows[0]
    halo_tiles = tile_bank[halo_banks[0]]
    source_ids = lax.broadcasted_iota(jnp.int32, (domains, slot_count), 0)
    gathered_ids = source_ids * pub_count + jnp.maximum(incoming, 0)

    def forward_tiles(position, running):
        column = lax.dynamic_index_in_dim(cols_here, position, 1, keepdims=False)
        bank_ids = lax.dynamic_index_in_dim(banks_here, position, 1, keepdims=False)
        return running + jnp.einsum(
            "rij,rjf->rif",
            tile_bank[bank_ids],
            feat_blocks[column],
            preferred_element_type=jnp.float32,
        )

    running = lax.fori_loop(
        0, tiles_row, forward_tiles, jnp.zeros((blocks, tile_size, narrow), jnp.float32)
    )
    shared = feat_blocks[own_pub]
    everyone = lax.all_gather(shared, "dom", axis=0, tiled=True)
    remote = everyone[gathered_ids]
    halo_terms = (
        jnp.einsum("dsij,dsjf->dsif", halo_tiles, remote, preferred_element_type=jnp.float32)
        * live_in
    )
    running = running + jax.ops.segment_sum(
        halo_terms.reshape(domains * slot_count, tile_size, narrow),
        rows_in.reshape(-1),
        num_segments=blocks,
    )
    agg_narrow = running.astype(jnp.bfloat16).reshape(part_rows, narrow)
    aggregated = lax.all_to_all(agg_narrow, "grp", split_axis=0, concat_axis=1, tiled=True)
    pre_act = jnp.dot(aggregated, weight, preferred_element_type=jnp.float32) + bias
    activations = jnp.maximum(pre_act, 0.0).astype(jnp.bfloat16)
    grad_pre = jnp.where(pre_act > 0, cotangent.astype(jnp.float32), 0.0).astype(jnp.bfloat16)
    weight_part = lax.dot_general(
        aggregated, grad_pre, (((0,), (0,)), ((), ())), preferred_element_type=jnp.float32
    )
    bias_part = jnp.sum(grad_pre.astype(jnp.float32), axis=0)
    grad_agg = lax.dot_general(
        grad_pre, weight, (((1,), (1,)), ((), ())), preferred_element_type=jnp.float32
    ).astype(jnp.bfloat16)
    grad_narrow = lax.all_to_all(grad_agg, "grp", split_axis=1, concat_axis=0, tiled=True)
    grad_blocks = grad_narrow.reshape(blocks, tile_size, narrow)

    def backward_tiles(position, running):
        column = lax.dynamic_index_in_dim(cols_here, position, 1, keepdims=False)
        bank_ids = lax.dynamic_index_in_dim(banks_here, position, 1, keepdims=False)
        contrib = jnp.einsum(
            "rji,rjf->rif", tile_bank[bank_ids], grad_blocks, preferred_element_type=jnp.float32
        )
        return running + jax.ops.segment_sum(contrib, column, num_segments=blocks)

    grad_total = lax.fori_loop(
        0, tiles_row, backward_tiles, jnp.zeros((blocks, tile_size, narrow), jnp.float32)
    )
    back_terms = (
        jnp.einsum(
            "dsji,dsjf->dsif", halo_tiles, grad_blocks[rows_in], preferred_element_type=jnp.float32
        )
        * live_in
    )
    placed = jax.ops.segment_sum(
        back_terms.reshape(domains * slot_count, tile_size, narrow),
        gathered_ids.reshape(-1),
        num_segments=domains * pub_count,
    )
    mine_back = lax.psum_scatter(placed, "dom", scatter_dimension=0, tiled=True)
    back_total = jax.ops.segment_sum(mine_back, own_pub, num_segments=blocks)
    grad_total = grad_total + back_total
    grad_nodes = lax.all_to_all(
        grad_total.astype(jnp.bfloat16).reshape(part_rows, narrow),
        "grp",
        split_axis=0,
        concat_axis=1,
        tiled=True,
    )
    norm_scale = float(rows_here * groups * domains) ** (-0.5)
    weight_total, bias_total = lax.psum((weight_part, bias_part), ("dom", "grp"))
    return (activations, grad_nodes, weight_total * norm_scale, bias_total * norm_scale)


def solution(mesh):
    in_specs = (
        P(("dom", "grp"), None),
        P(),
        P(),
        P(("dom", "grp"), None),
        P(),
        P("dom", None, None),
        P("dom", None, None),
        P("dom", None),
        P(),
        P("dom", None, None),
        P("dom", None, None),
    )
    out_specs = (P(("dom", "grp"), None), P(("dom", "grp"), None), P(), P())
    return jax.shard_map(
        per_device, mesh=mesh, in_specs=in_specs, out_specs=out_specs, check_vma=False
    )
```

profile of v0, /device:TPU:2, one launch (start us, length us, event | category | flops | bytes accessed | tf_op | source)
XLA Modules:
  0.0 686.9 jit_solution(15913844381797116386)
XLA Ops:
  7.2 2.0 copy_bitcast_fusion.1
  9.3 4.5 all-to-all-start
  14.9 2.1 gather_fusion.3
  17.1 7.1 %all-to-all-done = bf16[256,8,128]{2,0,1:T(8,128)(2,1)} async-done(((bf16[256,8,128]{2,0,1:T(8,128)(2,1)}), bf16[256,8,128]{2,0,1:T(8,128)(2,1)}, u32[]{:S(2)}, u32[]{:S(2)}) %all-to-all-start) | async-done | bytes 524320 | tf_op jit(solution)/shard_map/all_to_all | solution.py:28
  24.2 2.3 gather_fusion.4
  26.5 74.0 %while.28 = (s32[]{:T(128)}, f32[16,128,128]{2,1,0:T(8,128)S(1)}, s32[16,16]{0,1:T(8,128)S(1)}, bf16[16,128,128]{2,1,0:T(8,128)(2,1)S(1)}, s32[16,16]{0,1:T(8,12...) while((s32[]{:T(128)}, f32[16,128,128]{2,1,0:T(8,128)S(1)}, ...), condition=%wide.region_1.2_spmd.clone, body=%wide.region_0.1_spmd.clone.sunk | while | flops 67635296 | bytes 5251683 | solution.py:52
  27.2 2.4 gather_fusion.2
  31.8 2.4 gather_fusion.2
  36.4 2.4 gather_fusion.2
  38.9 1.5 convolution_add_fusion.3
  41.1 2.4 gather_fusion.2
  43.5 1.4 convolution_add_fusion.3
  45.7 2.5 gather_fusion.2
  48.2 1.4 convolution_add_fusion.3
  50.3 2.4 gather_fusion.2
  52.8 1.5 convolution_add_fusion.3
  55.0 2.4 gather_fusion.2
  59.6 2.4 gather_fusion.2
  64.2 2.4 gather_fusion.2
  68.8 2.4 gather_fusion.2
  73.4 2.4 gather_fusion.2
  78.1 2.4 gather_fusion.2
  82.7 2.5 gather_fusion.2
  87.3 2.4 gather_fusion.2
  91.9 2.5 gather_fusion.2
  96.6 2.4 gather_fusion.2
  99.0 1.5 convolution_add_fusion.3
  100.5 7.6 %all-gather.3.cloned.1.call-done = bf16[128,128,128]{2,1,0:T(8,128)(2,1)} async-done(((bf16[4,128,128]{2,1,0:T(8,128)(2,1)}), bf16[128,128,128]{2,1,0:T(8,128)(2,1)}) %all-gather.3.cloned.1.call-update) | async-done | bytes 4194320 | tf_op jit(solution)/shard_map/all_gather | solution.py:56
  108.1 4.3 gather_fusion.5
  112.4 4.9 convolution_multiply_fusion.1
  117.2 8.8 %scatter_fusion.1 = f32[16,128,128]{2,1,0:T(8,128)S(1)} fusion(f32[16,128,128]{2,1,0:T(8,128)S(1)} %get-tuple-element.222, s32[64]{0:T(128)S(1)} %reshape.272, f32[64,128,128]{2,1,0:T(8,128)} %bitcast.94), kind=kCustom, calls=%fused_computation.8 | custom fusion | flops 1048576 | bytes 12583168 | tf_op jit(solution)/shard_map/scatter-add | solution.py:62
  126.9 4.4 all-to-all-start.1
  131.6 10.1 %all-to-all-done.1 = bf16[8,256,128]{2,1,0:T(8,128)(2,1)S(1)} async-done(((bf16[8,256,128]{2,1,0:T(8,128)(2,1)}), bf16[8,256,128]{2,1,0:T(8,128)(2,1)S(1)}, u32[]{:S(2)}, u32[]{:S(2)}) %all-to-all-start.1) | async-done | bytes 524320 | tf_op jit(solution)/shard_map/all_to_all | solution.py:68
  144.6 3.5 all-to-all-start.2
  148.6 9.8 %all-to-all-done.2 = bf16[256,8,128]{2,0,1:T(8,128)(2,1)S(1)} async-done(((bf16[256,8,128]{2,0,1:T(8,128)(2,1)}), bf16[256,8,128]{2,0,1:T(8,128)(2,1)S(1)}, u32[]{:S(2)}, u32[]{:S(2)}) %all-to-all-start.2) | async-done | bytes 524320 | tf_op jit(solution)/shard_map/all_to_all | solution.py:79
  158.4 2.2 gather_fusion.6
  160.5 5.2 convolution_multiply_fusion
  165.8 4.3 broadcast_in_dim.12
  170.0 13.4 %scatter_fusion.2 = f32[128,128,128]{2,1,0:T(8,128)} fusion(f32[128,128,128]{2,1,0:T(8,128)} %broadcast_in_dim.12, s32[64]{0:T(128)S(1)} %add_bitcast_fusion, f32[64,128,128]{2,1,0:T(8,128)} %bitcast.93), kind=kCustom, calls=%fused_computation.9 | custom fusion | flops 1048576 | bytes 12583168 | tf_op jit(solution)/shard_map/scatter-add | solution.py:99
  183.5 75.8 %psum.15 = f32[512]{0:T(512)S(1)} all-reduce(f32[512]{0:T(512)S(1)} %get-tuple-element.277), channel_id=1, replica_groups=mesh['dom'=32,'grp'=8] {'dom','grp'}, use_global_device_ids=true, to_apply=%region_11.12 | all-reduce | flops 512 | bytes 4096 | tf_op jit(solution)/shard_map/psum | solution.py:115
  259.3 1.8 fusion.7
  262.2 98.2 %while.27 = (s32[]{:T(128)}, f32[16,128,128]{2,1,0:T(8,128)}, s32[16,16]{0,1:T(8,128)S(1)}, s32[16,16]{0,1:T(8,128)S(1)}, bf16[16,128,128]{2,1,0:T(8,128)(2,1)S(...) while((s32[]{:T(128)}, f32[16,128,128]{2,1,0:T(8,128)}, s32[16,16]{0,1:T(8,128)S(1)}, ...), condition=%wide.region_5.6_spmd, body=%wide.region_3.5_spmd.sunk | while | flops 67372080 | bytes 6296081 | solution.py:90
  265.0 3.3 scatter_fusion
  271.2 3.3 scatter_fusion
  277.3 3.3 scatter_fusion
  283.4 3.3 scatter_fusion
  289.6 3.3 scatter_fusion
  295.7 3.3 scatter_fusion
  301.9 3.3 scatter_fusion
  308.1 3.3 scatter_fusion
  314.2 3.3 scatter_fusion
  320.3 3.4 scatter_fusion
  326.5 3.3 scatter_fusion
  332.7 3.3 scatter_fusion
  338.8 3.3 scatter_fusion
  344.9 3.3 scatter_fusion
  351.0 3.3 scatter_fusion
  357.1 3.3 scatter_fusion
  360.4 48.2 %reduce-scatter.2.cloned.1.call-done = f32[4,128,128]{2,1,0:T(8,128)} async-done(((f32[128,128,128]{2,1,0:T(8,128)}), f32[4,128,128]{2,1,0:T(8,128)}) %reduce-scatter.2.cloned.1.call-update) | async-done | bytes 262160 | tf_op jit(solution)/shard_map/reduce_scatter | solution.py:104
  408.7 2.5 scatter_fusion.3
  411.1 2.1 convert_element_type.38
  413.3 4.3 all-to-all-start.3
  418.1 257.9 %all-reduce.2.cloned.1.call-done = f32[1024,512]{1,0:T(8,128)} async-done(((f32[1024,512]{1,0:T(8,128)}), f32[1024,512]{1,0:T(8,128)}) %all-reduce.2.cloned.1.call-update) | async-done | bytes 2097168 | tf_op jit(solution)/shard_map/psum | solution.py:115
  676.0 3.1 broadcast_multiply_fusion
  (206 shorter events, 80.1 us)
Async XLA Ops:
  7.2 134.8 %copy-start = (bf16[1024,512]{1,0:T(8,128)(2,1)S(1)}, bf16[1024,512]{1,0:T(8,128)(2,1)}, u32[]{:S(2)}) copy-start(bf16[1024,512]{1,0:T(8,128)(2,1)} %param.16) | copy-start | bytes 3145732
  7.2 6.6 copy-start.3
  7.2 6.8 copy-start.8
  7.2 7.4 %copy-start.4 = (s32[1,16,16]{2,1,0:T(8,128)S(1)}, s32[1,16,16]{2,1,0:T(8,128)}, u32[]{:S(2)}) copy-start(s32[1,16,16]{2,1,0:T(8,128)} %param.21) | copy-start | bytes 3076
  7.2 7.4 %copy-start.5 = (s32[1,16,16]{2,1,0:T(8,128)S(1)}, s32[1,16,16]{2,1,0:T(8,128)}, u32[]{:S(2)}) copy-start(s32[1,16,16]{2,1,0:T(8,128)} %param.20) | copy-start | bytes 3076
  7.2 7.5 %copy-start.6 = (s32[1,32,2]{1,2,0:T(2,128)S(1)}, s32[1,32,2]{1,2,0:T(2,128)}, u32[]{:S(2)}) copy-start(s32[1,32,2]{1,2,0:T(2,128)} %param.24) | copy-start | bytes 772
  7.2 7.7 %copy-start.1 = (bf16[16,128,128]{2,1,0:T(8,128)(2,1)S(1)}, bf16[16,128,128]{2,1,0:T(8,128)(2,1)}, u32[]{:S(2)}) copy-start(bf16[16,128,128]{2,1,0:T(8,128)(2,1)} %param.19) | copy-start | bytes 1572868
  9.3 14.9 %all-to-all-start = ((bf16[256,8,128]{2,0,1:T(8,128)(2,1)}), bf16[256,8,128]{2,0,1:T(8,128)(2,1)}, u32[]{:S(2)}, u32[]{:S(2)}) async-start(bf16[256,8,128]{2,0,1:T(8,128)(2,1)} %copy_bitcast_fusion.1), calls=%async_computation | async-start | bytes 1048576 | tf_op jit(solution)/shard_map/all_to_all | solution.py:28
  13.8 94.3 %all-gather.3.cloned.1.call-start = ((), (), s32[]{:S(2)}) async-start(), calls=%async_computation.7 | async-start | bytes 4325376 | tf_op jit(solution)/shard_map/all_gather | solution.py:56
  14.9 2.2 copy-start.9
  126.0 15.9 %copy-start.7 = (f32[512]{0:T(512)S(1)}, f32[512]{0:T(512)}, u32[]{:S(2)}) copy-start(f32[512]{0:T(512)} %param.17) | copy-start | bytes 6148
  126.9 16.2 %copy-start.2 = (bf16[256,512]{1,0:T(8,128)(2,1)S(1)}, bf16[256,512]{1,0:T(8,128)(2,1)}, u32[]{:S(2)}) copy-start(bf16[256,512]{1,0:T(8,128)(2,1)} %param.18) | copy-start | bytes 786436
  126.9 14.8 %all-to-all-start.1 = ((bf16[8,256,128]{2,1,0:T(8,128)(2,1)}), bf16[8,256,128]{2,1,0:T(8,128)(2,1)S(1)}, u32[]{:S(2)}, u32[]{:S(2)}) async-start(bf16[8,256,128]{2,1,0:T(8,128)(2,1)} %bitcast.15), calls=%async_computation.1 | async-start | bytes 1048576 | tf_op jit(solution)/shard_map/all_to_all | solution.py:68
  144.6 13.8 %all-to-all-start.2 = ((bf16[256,8,128]{2,0,1:T(8,128)(2,1)}), bf16[256,8,128]{2,0,1:T(8,128)(2,1)S(1)}, u32[]{:S(2)}, u32[]{:S(2)}) async-start(bf16[256,8,128]{2,0,1:T(8,128)(2,1)} %bitcast.76), calls=%async_computation.2 | async-start | bytes 1048576 | tf_op jit(solution)/shard_map/all_to_all | solution.py:79
  148.1 260.6 %reduce-scatter.2.cloned.1.call-start = ((), (), s32[]{:S(2)}) async-start(), calls=%async_computation.5 | async-start | bytes 8650752 | tf_op jit(solution)/shard_map/reduce_scatter | solution.py:104
  183.5 492.5 %all-reduce.2.cloned.1.call-start = ((), (), s32[]{:S(2)}) async-start(), calls=%async_computation.6 | async-start | bytes 4194304 | tf_op jit(solution)/shard_map/psum | solution.py:115
  413.3 265.9 %all-to-all-start.3 = ((bf16[8,256,128]{2,1,0:T(8,128)(2,1)}), bf16[8,256,128]{2,1,0:T(8,128)(2,1)S(1)}, u32[]{:S(2)}, u32[]{:S(2)}) async-start(bf16[8,256,128]{2,1,0:T(8,128)(2,1)} %bitcast.26), calls=%async_computation.4 | async-start | bytes 1048576 | tf_op jit(solution)/shard_map/all_to_all | solution.py:107
Sparse Core Ops, SparseCore 0:
  26.6 81.3 all-gather.2
  183.6 225.0 reduce-scatter.1
  415.5 260.4 all-reduce.1
where the time goes:
time: 691 us; the launch traced here: 687 us
  waiting for transfers between devices  341 us (49%)
  local copies, waits for them, and re-layouts  94.3 us (14%)
  other arithmetic  85.3 us (12%)
  blocking collectives  75.8 us (11%)
  matrix products  58.9 us (9%)
  starting transfers between devices  16.8 us (2%)
  between operations  14 us (2%)
    psum x1, waiting for transfers between devices, per_device(): lax.psum((weight_part, bias_part), ('dom', 'grp'))  258 us
    psum x1, blocking collectives, per_device(): lax.psum((weight_part, bias_part), ('dom', 'grp'))  75.8 us
    scatter-add x16, other arithmetic, backward_tiles(): return running + jax.ops.segment_sum(contrib, column, num_segments=blocks)  53.1 us
    reduce_scatter x1, waiting for transfers between devices, per_device(): mine_back = lax.psum_scatter(placed, 'dom', scatter_dimension=0, tiled=True)  48.2 us
    gather x16, local copies, waits for them, and re-layouts, forward_tiles(): feat_blocks[column]  39.2 us
    dot_general x16, matrix products, forward_tiles(): jnp.einsum('rij,rjf->rif', tile_bank[bank_ids], feat_blocks[column], pref...  23.2 us
    gather x16, local copies, waits for them, and re-layouts, backward_tiles(): tile_bank[bank_ids]  22.5 us
    dot_general x16, matrix products, backward_tiles(): jnp.einsum('rji,rjf->rif', tile_bank[bank_ids], grad_blocks, preferred_el...  22.3 us
  transfers between devices with their start and end apart: 7, of which 6 were waited for; matrix products, arithmetic and copies ran while one was open for 27% of the time, Pallas kernels for 0%

commit v1 on v0

--- a/solution.py
+++ b/solution.py
@@ -65,7 +65,10 @@
         num_segments=blocks,
     )
     agg_narrow = running.astype(jnp.bfloat16).reshape(part_rows, narrow)
-    aggregated = lax.all_to_all(agg_narrow, "grp", split_axis=0, concat_axis=1, tiled=True)
+    aggregated = jnp.concatenate(
+        lax.all_to_all(jnp.stack(jnp.split(agg_narrow, lax.axis_size("grp"), axis=0)), "grp", 0, 0),
+        axis=1,
+    )
     pre_act = jnp.dot(aggregated, weight, preferred_element_type=jnp.float32) + bias
     activations = jnp.maximum(pre_act, 0.0).astype(jnp.bfloat16)
     grad_pre = jnp.where(pre_act > 0, cotangent.astype(jnp.float32), 0.0).astype(jnp.bfloat16)

time: 691 us -> 696 us (level)
  no operation moved by 1% of the time
where the time goes in v1:
time: 696 us; the launch traced here: 692 us
  waiting for transfers between devices  341 us (49%)
  local copies, waits for them, and re-layouts  100 us (14%)
  other arithmetic  84.9 us (12%)
  blocking collectives  75.7 us (11%)
  matrix products  58.9 us (8%)
  starting transfers between devices  16.7 us (2%)
  between operations  14.1 us (2%)
    psum x1, waiting for transfers between devices, per_device(): lax.psum((weight_part, bias_part), ('dom', 'grp'))  258 us
    psum x1, blocking collectives, per_device(): lax.psum((weight_part, bias_part), ('dom', 'grp'))  75.7 us
    scatter-add x16, other arithmetic, backward_tiles(): return running + jax.ops.segment_sum(contrib, column, num_segments=blocks)  53.5 us
    reduce_scatter x1, waiting for transfers between devices, per_device(): mine_back = lax.psum_scatter(placed, 'dom', scatter_dimension=0, tiled=True)  47.9 us
    gather x16, local copies, waits for them, and re-layouts, forward_tiles(): feat_blocks[column]  39.2 us
    dot_general x16, matrix products, forward_tiles(): jnp.einsum('rij,rjf->rif', tile_bank[bank_ids], feat_blocks[column], pref...  23.2 us
    gather x16, local copies, waits for them, and re-layouts, backward_tiles(): tile_bank[bank_ids]  22.5 us
    dot_general x16, matrix products, backward_tiles(): jnp.einsum('rji,rjf->rif', tile_bank[bank_ids], grad_blocks, preferred_el...  22.3 us
  transfers between devices with their start and end apart: 7, of which 6 were waited for; matrix products, arithmetic and copies ran while one was open for 27% of the time, Pallas kernels for 0%

profile of v1, /device:TPU:2, one launch (start us, length us, event | category | flops | bytes accessed | tf_op | source)
XLA Modules:
  0.0 692.0 jit_solution(1476065796759474951)
XLA Ops:
  7.2 2.0 copy_bitcast_fusion.1
  9.3 4.5 all-to-all-start
  14.9 2.1 gather_fusion.3
  17.1 7.1 %all-to-all-done = bf16[256,8,128]{2,0,1:T(8,128)(2,1)} async-done(((bf16[256,8,128]{2,0,1:T(8,128)(2,1)}), bf16[256,8,128]{2,0,1:T(8,128)(2,1)}, u32[]{:S(2)}, u32[]{:S(2)}) %all-to-all-start) | async-done | bytes 524320 | tf_op jit(solution)/shard_map/all_to_all | solution.py:28
  24.2 2.3 gather_fusion.4
  26.5 74.0 %while.28 = (s32[]{:T(128)}, f32[16,128,128]{2,1,0:T(8,128)S(1)}, s32[16,16]{0,1:T(8,128)S(1)}, bf16[16,128,128]{2,1,0:T(8,128)(2,1)S(1)}, s32[16,16]{0,1:T(8,12...) while((s32[]{:T(128)}, f32[16,128,128]{2,1,0:T(8,128)S(1)}, ...), condition=%wide.region_1.2_spmd.clone, body=%wide.region_0.1_spmd.clone.sunk | while | flops 67635296 | bytes 5251683 | solution.py:52
  27.2 2.4 gather_fusion.2
  31.8 2.4 gather_fusion.2
  36.4 2.4 gather_fusion.2
  38.9 1.5 convolution_add_fusion.3
  41.1 2.4 gather_fusion.2
  43.5 1.4 convolution_add_fusion.3
  45.7 2.5 gather_fusion.2
  48.2 1.4 convolution_add_fusion.3
  50.3 2.4 gather_fusion.2
  52.8 1.5 convolution_add_fusion.3
  55.0 2.4 gather_fusion.2
  59.6 2.4 gather_fusion.2
  64.2 2.4 gather_fusion.2
  68.8 2.4 gather_fusion.2
  73.4 2.4 gather_fusion.2
  78.1 2.4 gather_fusion.2
  82.7 2.5 gather_fusion.2
  87.3 2.4 gather_fusion.2
  91.9 2.5 gather_fusion.2
  96.6 2.4 gather_fusion.2
  99.0 1.5 convolution_add_fusion.3
  100.5 7.6 %all-gather.3.cloned.1.call-done = bf16[128,128,128]{2,1,0:T(8,128)(2,1)} async-done(((bf16[4,128,128]{2,1,0:T(8,128)(2,1)}), bf16[128,128,128]{2,1,0:T(8,128)(2,1)}) %all-gather.3.cloned.1.call-update) | async-done | bytes 4194320 | tf_op jit(solution)/shard_map/all_gather | solution.py:56
  108.1 4.3 gather_fusion.5
  112.4 4.9 convolution_multiply_fusion.1
  117.3 8.8 %scatter_fusion.1 = f32[16,128,128]{2,1,0:T(8,128)S(1)} fusion(f32[16,128,128]{2,1,0:T(8,128)S(1)} %get-tuple-element.222, s32[64]{0:T(128)S(1)} %reshape.292, f32[64,128,128]{2,1,0:T(8,128)} %bitcast.102), kind=kCustom, calls=%fused_computation.8 | custom fusion | flops 1048576 | bytes 12583168 | tf_op jit(solution)/shard_map/scatter-add | solution.py:62
  132.2 4.3 all-to-all-start.1
  136.7 10.1 %all-to-all-done.1 = bf16[8,256,128]{1,2,0:T(8,128)(2,1)S(1)} async-done(((bf16[8,256,128]{1,2,0:T(8,128)(2,1)}), bf16[8,256,128]{1,2,0:T(8,128)(2,1)S(1)}, u32[]{:S(2)}, u32[]{:S(2)}) %all-to-all-start.1) | async-done | bytes 524320 | tf_op jit(solution)/shard_map/all_to_all | solution.py:69
  149.5 3.5 all-to-all-start.2
  153.5 9.8 %all-to-all-done.2 = bf16[256,8,128]{2,0,1:T(8,128)(2,1)S(1)} async-done(((bf16[256,8,128]{2,0,1:T(8,128)(2,1)}), bf16[256,8,128]{2,0,1:T(8,128)(2,1)S(1)}, u32[]{:S(2)}, u32[]{:S(2)}) %all-to-all-start.2) | async-done | bytes 524320 | tf_op jit(solution)/shard_map/all_to_all | solution.py:82
  163.3 2.1 gather_fusion.6
  165.4 5.2 convolution_multiply_fusion
  170.6 4.3 broadcast_in_dim.12
  174.9 13.4 %scatter_fusion.2 = f32[128,128,128]{2,1,0:T(8,128)} fusion(f32[128,128,128]{2,1,0:T(8,128)} %broadcast_in_dim.12, s32[64]{0:T(128)S(1)} %add_bitcast_fusion, f32[64,128,128]{2,1,0:T(8,128)} %bitcast.101), kind=kCustom, calls=%fused_computation.9 | custom fusion | flops 1048576 | bytes 12583168 | tf_op jit(solution)/shard_map/scatter-add | solution.py:102
  188.4 75.7 %psum.15 = f32[512]{0:T(512)S(1)} all-reduce(f32[512]{0:T(512)S(1)} %get-tuple-element.277), channel_id=1, replica_groups=mesh['dom'=32,'grp'=8] {'dom','grp'}, use_global_device_ids=true, to_apply=%region_11.12 | all-reduce | flops 512 | bytes 4096 | tf_op jit(solution)/shard_map/psum | solution.py:118
  264.2 1.7 fusion.8
  267.0 98.7 %while.27 = (s32[]{:T(128)}, f32[16,128,128]{2,1,0:T(8,128)}, s32[16,16]{0,1:T(8,128)S(1)}, s32[16,16]{0,1:T(8,128)S(1)}, bf16[16,128,128]{2,1,0:T(8,128)(2,1)S(...) while((s32[]{:T(128)}, f32[16,128,128]{2,1,0:T(8,128)}, s32[16,16]{0,1:T(8,128)S(1)}, ...), condition=%wide.region_5.6_spmd, body=%wide.region_3.5_spmd.sunk | while | flops 67372080 | bytes 6296081 | solution.py:93
  269.9 3.4 scatter_fusion
  276.0 3.3 scatter_fusion
  282.2 3.3 scatter_fusion
  288.4 3.4 scatter_fusion
  294.6 3.4 scatter_fusion
  300.8 3.3 scatter_fusion
  307.0 3.3 scatter_fusion
  313.2 3.4 scatter_fusion
  319.3 3.3 scatter_fusion
  325.5 3.4 scatter_fusion
  331.7 3.3 scatter_fusion
  337.8 3.3 scatter_fusion
  344.0 3.3 scatter_fusion
  350.1 3.3 scatter_fusion
  356.2 3.3 scatter_fusion
  362.4 3.3 scatter_fusion
  365.7 47.9 %reduce-scatter.2.cloned.1.call-done = f32[4,128,128]{2,1,0:T(8,128)} async-done(((f32[128,128,128]{2,1,0:T(8,128)}), f32[4,128,128]{2,1,0:T(8,128)}) %reduce-scatter.2.cloned.1.call-update) | async-done | bytes 262160 | tf_op jit(solution)/shard_map/reduce_scatter | solution.py:107
  413.6 2.5 scatter_fusion.3
  416.1 2.1 convert_element_type.38
  418.2 4.3 all-to-all-start.3
  423.1 258.0 %all-reduce.2.cloned.1.call-done = f32[1024,512]{1,0:T(8,128)} async-done(((f32[1024,512]{1,0:T(8,128)}), f32[1024,512]{1,0:T(8,128)}) %all-reduce.2.cloned.1.call-update) | async-done | bytes 2097168 | tf_op jit(solution)/shard_map/psum | solution.py:118
  681.1 3.1 broadcast_multiply_fusion
  (222 shorter events, 85.1 us)
Async XLA Ops:
  7.2 139.7 %copy-start = (bf16[1024,512]{1,0:T(8,128)(2,1)S(1)}, bf16[1024,512]{1,0:T(8,128)(2,1)}, u32[]{:S(2)}) copy-start(bf16[1024,512]{1,0:T(8,128)(2,1)} %param.16) | copy-start | bytes 3145732
  7.2 6.6 copy-start.3
  7.2 6.8 copy-start.8
  7.2 7.4 %copy-start.4 = (s32[1,16,16]{2,1,0:T(8,128)S(1)}, s32[1,16,16]{2,1,0:T(8,128)}, u32[]{:S(2)}) copy-start(s32[1,16,16]{2,1,0:T(8,128)} %param.21) | copy-start | bytes 3076
  7.2 7.4 %copy-start.5 = (s32[1,16,16]{2,1,0:T(8,128)S(1)}, s32[1,16,16]{2,1,0:T(8,128)}, u32[]{:S(2)}) copy-start(s32[1,16,16]{2,1,0:T(8,128)} %param.20) | copy-start | bytes 3076
  7.2 7.5 %copy-start.6 = (s32[1,32,2]{1,2,0:T(2,128)S(1)}, s32[1,32,2]{1,2,0:T(2,128)}, u32[]{:S(2)}) copy-start(s32[1,32,2]{1,2,0:T(2,128)} %param.24) | copy-start | bytes 772
  7.2 7.7 %copy-start.1 = (bf16[16,128,128]{2,1,0:T(8,128)(2,1)S(1)}, bf16[16,128,128]{2,1,0:T(8,128)(2,1)}, u32[]{:S(2)}) copy-start(bf16[16,128,128]{2,1,0:T(8,128)(2,1)} %param.19) | copy-start | bytes 1572868
  9.3 14.9 %all-to-all-start = ((bf16[256,8,128]{2,0,1:T(8,128)(2,1)}), bf16[256,8,128]{2,0,1:T(8,128)(2,1)}, u32[]{:S(2)}, u32[]{:S(2)}) async-start(bf16[256,8,128]{2,0,1:T(8,128)(2,1)} %copy_bitcast_fusion.1), calls=%async_computation | async-start | bytes 1048576 | tf_op jit(solution)/shard_map/all_to_all | solution.py:28
  13.8 94.3 %all-gather.3.cloned.1.call-start = ((), (), s32[]{:S(2)}) async-start(), calls=%async_computation.7 | async-start | bytes 4325376 | tf_op jit(solution)/shard_map/all_gather | solution.py:56
  14.9 2.2 copy-start.9
  126.1 20.7 %copy-start.7 = (f32[512]{0:T(512)S(1)}, f32[512]{0:T(512)}, u32[]{:S(2)}) copy-start(f32[512]{0:T(512)} %param.17) | copy-start | bytes 6148
  128.4 19.6 %copy-start.2 = (bf16[256,512]{1,0:T(8,128)(2,1)S(1)}, bf16[256,512]{1,0:T(8,128)(2,1)}, u32[]{:S(2)}) copy-start(bf16[256,512]{1,0:T(8,128)(2,1)} %param.18) | copy-start | bytes 786436
  132.2 14.6 %all-to-all-start.1 = ((bf16[8,256,128]{1,2,0:T(8,128)(2,1)}), bf16[8,256,128]{1,2,0:T(8,128)(2,1)S(1)}, u32[]{:S(2)}, u32[]{:S(2)}) async-start(bf16[8,256,128]{1,2,0:T(8,128)(2,1)} %constant_dynamic-update-slice_fusion), calls=%async_computation.1 | async-start | bytes 1048576 | tf_op jit(solution)/shard_map/all_to_all | solution.py:69
  149.5 13.8 %all-to-all-start.2 = ((bf16[256,8,128]{2,0,1:T(8,128)(2,1)}), bf16[256,8,128]{2,0,1:T(8,128)(2,1)S(1)}, u32[]{:S(2)}, u32[]{:S(2)}) async-start(bf16[256,8,128]{2,0,1:T(8,128)(2,1)} %bitcast.84), calls=%async_computation.2 | async-start | bytes 1048576 | tf_op jit(solution)/shard_map/all_to_all | solution.py:82
  153.0 260.6 %reduce-scatter.2.cloned.1.call-start = ((), (), s32[]{:S(2)}) async-start(), calls=%async_computation.5 | async-start | bytes 8650752 | tf_op jit(solution)/shard_map/reduce_scatter | solution.py:107
  188.4 492.7 %all-reduce.2.cloned.1.call-start = ((), (), s32[]{:S(2)}) async-start(), calls=%async_computation.6 | async-start | bytes 4194304 | tf_op jit(solution)/shard_map/psum | solution.py:118
  418.2 266.1 %all-to-all-start.3 = ((bf16[8,256,128]{2,1,0:T(8,128)(2,1)}), bf16[8,256,128]{2,1,0:T(8,128)(2,1)S(1)}, u32[]{:S(2)}, u32[]{:S(2)}) async-start(bf16[8,256,128]{2,1,0:T(8,128)(2,1)} %bitcast.33), calls=%async_computation.4 | async-start | bytes 1048576 | tf_op jit(solution)/shard_map/all_to_all | solution.py:110
Sparse Core Ops, SparseCore 0:
  26.6 81.3 all-gather.2
  188.5 225.0 reduce-scatter.1
  420.5 260.6 all-reduce.1
